TPU v7x, 32 devices: a whole 2x2x4 slice. The times are simulated.
32 devices in a mesh: groups: 2 (over x), gx: 16 (over z, y, core).
Axes of the slice: x: 2, y: 2, z: 4, core: 2. Of those that a mesh axis runs over, the one named last changes fastest.
Arguments:
- volume: bfloat16 [32, 64, 16, 256], P(None, ('groups', 'gx')), parts along dimension 1, may hold values from -6 to 6
- weight_two: bfloat16 [32, 32, 3, 3, 3], replicated, may hold values from -0.21875 to 0.21875
- weight_three: bfloat16 [64, 32, 3, 3, 3], replicated, may hold values from -0.21875 to 0.21875
- cotangent: bfloat16 [64, 32, 8, 128], P(None, ('groups', 'gx')), parts along dimension 1, may hold values from -6 to 6
Outputs:
- features_three: bfloat16 [64, 32, 8, 128], P(None, ('groups', 'gx')), parts along dimension 1
- grad_three: float32 [128, 32, 3, 3, 3], P(('groups', 'gx')), parts along dimension 0
- grad_two: float32 [64, 32, 3, 3, 3], P('groups'), parts along dimension 0
- grad_volume: bfloat16 [32, 64, 16, 256], P(None, ('groups', 'gx')), parts along dimension 1
There are 2 independent parts, one for each index of `groups`. A program takes and returns all parts, laid end to end along the dimension named above; an argument that names none is the same for every part. Nothing has to cross between parts.
All inputs are finite; a program needn't handle non-finite values.
Results may differ from a plain program's by a relative error of at most 0.012.
Values may be sent and summed in bfloat16 or wider, within the bound.
A program may use at most 128 MiB of HBM per device.

v0:
```python
import functools

import jax
import jax.numpy as jnp
from jax import lax
from jax.experimental import pallas as pl
from jax.experimental.pallas import tpu as pltpu
from jax.sharding import PartitionSpec as P

F32 = jnp.float32
BF16 = jnp.bfloat16
MESH = pl.DeviceIdType.MESH
NN = (((1,), (0,)), ((), ()))
NT = (((1,), (1,)), ((), ()))


def dot(a, b, dims=NN):
    return lax.dot_general(a, b, dims, preferred_element_type=F32)


def eye(n):
    return (
        lax.broadcasted_iota(jnp.int32, (n, n), 0) == lax.broadcasted_iota(jnp.int32, (n, n), 1)
    ).astype(BF16)


def lane_concat(ref):
    return jnp.concatenate([ref[t].astype(F32) for t in range(ref.shape[0])], axis=1).astype(BF16)


def shifts(x):
    width = x.shape[1]
    lane = lax.broadcasted_iota(jnp.int32, x.shape, 1)
    before = jnp.where(lane == 0, 0.0, pltpu.roll(x, 1, 1))
    after = jnp.where(lane == width - 1, 0.0, pltpu.roll(x, width - 1, 1))
    return before.astype(BF16), x.astype(BF16), after.astype(BF16)


def rows_first(ref, value):
    for i in range(ref.shape[0]):
        ref[i] = value[:, 128 * i : 128 * (i + 1)]


def joined(ref):
    return jnp.concatenate([ref[i] for i in range(ref.shape[0])], axis=1)


def strided(ref, start, count, step):
    parts = [ref[i, pl.ds(start, count, stride=step), :] for i in range(ref.shape[0])]
    return jnp.concatenate(parts, axis=1)


def put_strided(ref, start, step, value):
    for i in range(ref.shape[0]):
        ref[i, pl.ds(start, value.shape[0], stride=step), :] = value[:, 128 * i : 128 * (i + 1)]


def put_stack(stack, z, h, x, flip):
    c = x.shape[0]
    pieces = shifts(x)
    if flip:
        pieces = pieces[::-1]
    for i, piece in enumerate(pieces):
        stack[z, h + 1, i * c : (i + 1) * c, :] = piece


def zero_rims(stack):
    planes, rows, k, w = stack.shape
    for z in range(planes):
        stack[z, 0] = jnp.zeros((k, w), BF16)
        stack[z, rows - 1] = jnp.zeros((k, w), BF16)


def window(stack, base, h, flip):
    parts = []
    k, w = stack.shape[2:]
    for dz in (2, 1, 0) if flip else (0, 1, 2):
        slab = stack[base + dz, pl.ds(h, 3)]
        if flip:
            parts += [slab[2], slab[1], slab[0]]
        else:
            parts.append(slab.reshape(3 * k, w))
    return jnp.concatenate(parts, axis=0)


def kernel(
    n,
    vol, w2, w3, cot,
    feat, g3, g2, gvol,
    rv, rc, rp, rb, pown, bown,
    xs, xb, xp, xc, tv, tc, tf, slope,
    a2, b2, a3, b3, acc2, acc3,
    g2send, g2recv, g2ag, g3send, g3recv,
    halo_send, halo_recv, s2, r2, sa, ra, s3, r3,
):
    me = lax.axis_index("gx")
    chan, planes, height, width = vol.shape
    filt, _, height_half, width_half = cot.shape
    barrier = pltpu.get_barrier_semaphore()

    def peer(j):
        return lax.rem(me + j, n)

    def greet(j, carry):
        pl.semaphore_signal(barrier, inc=1, device_id={"gx": peer(j)}, device_id_type=MESH)
        return carry

    lax.fori_loop(1, n, greet, 0)
    pl.semaphore_wait(barrier, n - 1)

    def halo(slot, up, src, dst):
        index = 2 * slot + (0 if up else 1)
        return pltpu.make_async_remote_copy(
            src_ref=src,
            dst_ref=dst.at[0 if up else 1],
            send_sem=halo_send.at[index],
            recv_sem=halo_recv.at[index],
            device_id={"gx": lax.rem(me + (1 if up else n - 1), n)},
            device_id_type=MESH,
        )

    def halo_start(slot, first, last, dst):
        @pl.when(me < n - 1)
        def _():
            halo(slot, True, last, dst).start()

        @pl.when(me > 0)
        def _():
            halo(slot, False, first, dst).start()

    def halo_arrive(slot, first, last, dst):
        @pl.when(me > 0)
        def _():
            halo(slot, True, last, dst).wait_recv()

        @pl.when(me < n - 1)
        def _():
            halo(slot, False, first, dst).wait_recv()

    def halo_sent(slot, first, last, dst):
        @pl.when(me < n - 1)
        def _():
            halo(slot, True, last, dst).wait_send()

        @pl.when(me > 0)
        def _():
            halo(slot, False, first, dst).wait_send()

    halos = (
        (0, vol.at[:, 0], vol.at[:, planes - 1], rv),
        (1, cot.at[:, 0], cot.at[:, 0], rc),
        (2, pown, pown, rp),
        (3, bown.at[0], bown.at[planes - 1], rb),
    )
    halo_start(*halos[1])
    halo_start(*halos[0])

    @pl.when(me == 0)
    def _():
        for ref in (rv, rc, rp, rb):
            ref[0] = jnp.zeros(ref.shape[1:], BF16)

    @pl.when(me == n - 1)
    def _():
        for ref in (rv, rc, rp, rb):
            ref[1] = jnp.zeros(ref.shape[1:], BF16)

    for stack in (xs, xb, xp, xc):
        zero_rims(stack)
    a2[...] = lane_concat(w2)
    b3[...] = lane_concat(w3)
    b2[...] = dot(eye(chan), w2[...].reshape(-1, chan), NT).astype(BF16)
    a3[...] = dot(eye(filt), w3[...].reshape(-1, filt), NT).astype(BF16)

    def build_fine(value, z):
        rows_first(tv, value.astype(F32).reshape(chan * height, width))

        def row(h, carry):
            put_stack(xs, z, h, strided(tv, h, chan, height), False)
            return carry

        lax.fori_loop(0, height, row, 0)

    def build_cot(value, z):
        rows_first(tc, value.astype(F32).reshape(filt * height_half, width_half))

        def row(h, carry):
            put_stack(xc, z, h, strided(tc, h, filt, height_half), True)
            return carry

        lax.fori_loop(0, height_half, row, 0)

    build_cot(cot[:, 0], 1)
    for d in range(planes):
        build_fine(vol[:, d], d + 1)
    halo_arrive(*halos[1])
    build_cot(rc[0], 0)
    build_cot(rc[1], 2)
    halo_arrive(*halos[0])
    build_fine(rv[0], 0)
    build_fine(rv[1], planes + 1)

    fine = lax.broadcasted_iota(jnp.int32, (width, width_half), 0)
    coarse = lax.broadcasted_iota(jnp.int32, (width, width_half), 1)
    pool = ((fine == 2 * coarse) | (fine == 2 * coarse + 1)).astype(BF16)

    def forward(hc, carry):
        total = jnp.zeros((chan, width), F32)
        for d in range(planes):
            for e in range(2):
                h = 2 * hc + e
                before = dot(a2[...], window(xs, d, h, False))
                sigma = jax.nn.sigmoid(before)
                slope[d, h] = sigma * (1.0 + before * (1.0 - sigma)) * 0.125
                total = total + (before * sigma).astype(BF16).astype(F32)
        high = total.astype(BF16)
        low = (total - high.astype(F32)).astype(BF16)
        pooled = ((dot(high, pool) + dot(low, pool)) * 0.125).astype(BF16)
        pown[hc] = pooled
        put_stack(xp, 1, hc, pooled.astype(F32), False)
        return carry

    lax.fori_loop(0, height_half, forward, 0)
    halo_start(*halos[2])

    def backward(hc, carry):
        back = dot(b3[...], window(xc, 0, hc, True)).astype(BF16)
        spread = dot(back, pool, NT)
        for d in range(planes):
            for e in range(2):
                h = 2 * hc + e
                value = (spread * slope[d, h]).astype(BF16)
                bown[d, h] = value
                put_stack(xb, d + 1, h, value.astype(F32), True)
        return carry

    lax.fori_loop(0, height_half, backward, 0)
    halo_start(*halos[3])

    k2 = a2.shape[1]
    acc2[...] = jnp.zeros(acc2.shape, F32)

    def weight_two(h, carry):
        for d in range(planes):
            acc2[:, :k2] += dot(bown[d, h], window(xs, d, h, False), NT)
        return carry

    lax.fori_loop(0, height, weight_two, 0)

    rows = acc2.shape[0] // 8
    units = rows * (acc2.shape[1] // 128)
    per = g2send.shape[1] // 8

    def place(u):
        j, r = u // rows, u % rows
        return (slice(8 * r, 8 * r + 8), slice(128 * j, 128 * j + 128))

    for u in range(n * per):
        at = (u // per, slice(u % per * 8, u % per * 8 + 8))
        g2send[at] = acc2[place(u)] if u < units else jnp.zeros((8, 128), F32)

    def scatter(send, recv, ssem, rsem, k, s):
        return pltpu.make_async_remote_copy(
            src_ref=send.at[k],
            dst_ref=recv.at[s],
            send_sem=ssem.at[k],
            recv_sem=rsem.at[s],
            device_id={"gx": k},
            device_id_type=MESH,
        )

    def start_all(send, recv, ssem, rsem):
        def one(j, carry):
            scatter(send, recv, ssem, rsem, peer(j), me).start()
            return carry

        lax.fori_loop(1, n, one, 0)

    def wait_sends(send, recv, ssem, rsem):
        def one(j, carry):
            scatter(send, recv, ssem, rsem, peer(j), me).wait_send()
            return carry

        lax.fori_loop(1, n, one, 0)

    def sum_all(send, recv, ssem, rsem):
        def one(j, total):
            s = peer(j)
            scatter(send, recv, ssem, rsem, s, s).wait_recv()
            return total + recv[s]

        return lax.fori_loop(1, n, one, send[me])

    halo_arrive(*halos[2])
    for z in range(2):

        def pooled_row(h, carry, z=z):
            put_stack(xp, 2 * z, h, rp[z, h].astype(F32), False)
            return carry

        lax.fori_loop(0, height_half, pooled_row, 0)
    start_all(g2send, g2recv, s2, r2)

    acc3[...] = jnp.zeros(acc3.shape, F32)

    def weight_three(h, carry):
        acc3[...] += dot(xc[1, h + 1, filt : 2 * filt, :], window(xp, 0, h, False), NT)
        return carry

    lax.fori_loop(0, height_half, weight_three, 0)
    own = filt // n
    for i in range(n):
        g3send[i] = acc3[i * own : (i + 1) * own, :]

    def features(h, carry):
        put_strided(tf, h, height_half, dot(a3[...], window(xp, 0, h, False)))
        return carry

    lax.fori_loop(0, height_half, features, 0)
    feat[:, 0] = joined(tf).reshape(filt, height_half, width_half).astype(BF16)
    start_all(g3send, g3recv, s3, r3)

    g2ag[me] = sum_all(g2send, g2recv, s2, r2)

    halo_arrive(*halos[3])
    for z in range(2):

        def back_row(h, carry, z=z):
            put_stack(xb, (planes + 1) * z, h, rb[z, h].astype(F32), True)
            return carry

        lax.fori_loop(0, height, back_row, 0)

    def gather(k, s):
        return pltpu.make_async_remote_copy(
            src_ref=g2ag.at[s],
            dst_ref=g2ag.at[s],
            send_sem=sa.at[k],
            recv_sem=ra.at[s],
            device_id={"gx": k},
            device_id_type=MESH,
        )

    def gather_start(j, carry):
        gather(peer(j), me).start()
        return carry

    lax.fori_loop(1, n, gather_start, 0)

    for d in range(planes):

        def volume_row(h, carry, d=d):
            put_strided(tv, h, height, dot(b2[...], window(xb, d, h, True)))
            return carry

        lax.fori_loop(0, height, volume_row, 0)
        gvol[:, d] = joined(tv).reshape(chan, height, width).astype(BF16)

    taps = w2.shape[0]
    total = sum_all(g3send, g3recv, s3, r3)
    for t in range(taps):
        g3[t] = total[:, chan * t : chan * (t + 1)]

    def gather_wait(j, carry):
        gather(peer(j), peer(j)).wait_recv()
        return carry

    lax.fori_loop(1, n, gather_wait, 0)
    for u in range(units):
        acc2[place(u)] = g2ag[u // per, u % per * 8 : u % per * 8 + 8]
    for t in range(taps):
        g2[t] = acc2[:, chan * t : chan * (t + 1)]

    for item in halos:
        halo_sent(*item)
    wait_sends(g2send, g2recv, s2, r2)
    wait_sends(g3send, g3recv, s3, r3)

    def gather_sent(j, carry):
        gather(peer(j), me).wait_send()
        return carry

    lax.fori_loop(1, n, gather_sent, 0)


def local(n, volume, weight_two, weight_three, cotangent):
    chan, planes, height, width = volume.shape
    filt, _, height_half, width_half = cotangent.shape
    taps = 27
    w2 = jnp.transpose(weight_two, (2, 3, 4, 0, 1)).reshape(taps, chan, chan)
    w3 = jnp.transpose(weight_three, (2, 3, 4, 1, 0)).reshape(taps, chan, filt)
    k2 = taps * chan
    k2pad = -(-k2 // 128) * 128
    units = chan // 8 * (k2pad // 128)
    per = -(-units // n)
    own = filt // n
    dma = pltpu.SemaphoreType.DMA
    vmem = pl.BlockSpec(memory_space=pltpu.VMEM)
    feat, g3, g2, gvol = pl.pallas_call(
        functools.partial(kernel, n),
        out_shape=(
            jax.ShapeDtypeStruct(cotangent.shape, BF16),
            jax.ShapeDtypeStruct((taps, own, chan), F32),
            jax.ShapeDtypeStruct((taps, chan, chan), F32),
            jax.ShapeDtypeStruct(volume.shape, BF16),
        ),
        in_specs=[vmem] * 4,
        out_specs=(vmem,) * 4,
        scratch_shapes=[
            pltpu.VMEM((2, chan, height, width), BF16),
            pltpu.VMEM((2, filt, height_half, width_half), BF16),
            pltpu.VMEM((2, height_half, chan, width_half), BF16),
            pltpu.VMEM((2, height, chan, width), BF16),
            pltpu.VMEM((height_half, chan, width_half), BF16),
            pltpu.VMEM((planes, height, chan, width), BF16),
            pltpu.VMEM((planes + 2, height + 2, 3 * chan, width), BF16),
            pltpu.VMEM((planes + 2, height + 2, 3 * chan, width), BF16),
            pltpu.VMEM((3, height_half + 2, 3 * chan, width_half), BF16),
            pltpu.VMEM((3, height_half + 2, 3 * filt, width_half), BF16),
            pltpu.VMEM((width // 128, chan * height, 128), F32),
            pltpu.VMEM((width_half // 128, filt * height_half, 128), F32),
            pltpu.VMEM((width_half // 128, filt * height_half, 128), F32),
            pltpu.VMEM((planes, height, chan, width), F32),
            pltpu.VMEM((chan, k2), BF16),
            pltpu.VMEM((chan, k2), BF16),
            pltpu.VMEM((filt, k2), BF16),
            pltpu.VMEM((chan, taps * filt), BF16),
            pltpu.VMEM((chan, k2pad), F32),
            pltpu.VMEM((filt, k2), F32),
            pltpu.VMEM((n, per * 8, 128), F32),
            pltpu.VMEM((n, per * 8, 128), F32),
            pltpu.VMEM((n, per * 8, 128), F32),
            pltpu.VMEM((n, own, k2), F32),
            pltpu.VMEM((n, own, k2), F32),
            dma((8,)), dma((8,)),
            dma((n,)), dma((n,)), dma((n,)), dma((n,)), dma((n,)), dma((n,)),
        ],
        compiler_params=pltpu.CompilerParams(
            collective_id=0, has_side_effects=True, vmem_limit_bytes=48 << 20
        ),
    )(volume, w2, w3, cotangent)

    def taps_last(grad):
        return jnp.transpose(grad.reshape(3, 3, 3, *grad.shape[1:]), (3, 4, 0, 1, 2))

    return feat, taps_last(g3), taps_last(g2), gvol


def solution(mesh):
    return jax.shard_map(
        functools.partial(local, mesh.shape["gx"]),
        mesh=mesh,
        in_specs=(
            P(None, ("groups", "gx"), None, None),
            P(),
            P(),
            P(None, ("groups", "gx"), None, None),
        ),
        out_specs=(
            P(None, ("groups", "gx"), None, None),
            P(("groups", "gx"), None, None, None, None),
            P("groups", None, None, None, None),
            P(None, ("groups", "gx"), None, None),
        ),
        check_vma=False,
    )
```

profile of v0, /device:TPU:0, one launch (start us, length us, event | category | flops | bytes accessed | tf_op | source)
XLA Modules:
  0.0 57.6 jit_solution(13856463617873761278)
XLA Ops:
  0.6 0.0 copy-start
  0.6 1.0 %copy-done = bf16[32,2,16,256]{3,2,1,0:T(8,128)(2,1)S(1)} copy-done((bf16[32,2,16,256]{3,2,1,0:T(8,128)(2,1)S(1)}, bf16[32,2,16,256]{3,2,1,0:T(8,128)(2,1)}, u32[]{:S(2)}) %copy-start) | copy-done | bytes 524312
  1.7 0.0 copy-start.1
  1.7 0.9 %copy-done.1 = bf16[32,32,3,3,3]{1,0,4,3,2:T(8,128)(2,1)S(1)} copy-done((bf16[32,32,3,3,3]{1,0,4,3,2:T(8,128)(2,1)S(1)}, bf16[32,32,3,3,3]{1,0,4,3,2:T(8,128)(2,1)}, u32[]{:S(2)}) %copy-start.1) | copy-done | bytes 55320
  2.6 0.0 copy-start.2
  2.6 0.9 %copy-done.2 = bf16[64,32,3,3,3]{0,1,4,3,2:T(8,128)(2,1)S(1)} copy-done((bf16[64,32,3,3,3]{0,1,4,3,2:T(8,128)(2,1)S(1)}, bf16[64,32,3,3,3]{0,1,4,3,2:T(8,128)(2,1)}, u32[]{:S(2)}) %copy-start.2) | copy-done | bytes 110616
  3.5 0.0 copy-start.3
  3.5 0.9 %copy-done.3 = bf16[64,1,8,128]{3,2,1,0:T(8,128)(2,1)S(1)} copy-done((bf16[64,1,8,128]{3,2,1,0:T(8,128)(2,1)S(1)}, bf16[64,1,8,128]{3,2,1,0:T(8,128)(2,1)}, u32[]{:S(2)}) %copy-start.3) | copy-done | bytes 131096
  4.5 50.3 %shard_map.75 = (bf16[64,1,8,128]{3,2,1,0:T(8,128)(2,1)S(1)}, f32[27,4,32]{2,1,0:T(4,128)S(1)}, f32[27,32,32]{2,1,0:T(8,128)S(1)}, bf16[32,2,16,256]{3,2,1,0:T(8,128)(2,1)S(1)}) custom-call(bf16[32,2,16,256]{3,2,1,0:T(8,128)(2,1)S(1)} %copy-done, bf16[27,32,32]{2,1,0:T(8,128)(2,1)S(1)} %bitcast.13, bf16[27,32,64]{2,1,0:T(8,128)(2,1)S(1)} %bitcast.14, ...), custom_call_target="tpu_custom_call" | custom-call | tf_op jit(solution)/shard_map/pallas_call | solution.py:399
  54.7 0.7 %copy.12 = bf16[64,1,8,128]{3,2,1,0:T(8,128)(2,1)} copy(bf16[64,1,8,128]{3,2,1,0:T(8,128)(2,1)S(1)} %get-tuple-element.16) | data formatting | bytes 262144
  55.4 0.6 %copy.13 = f32[4,32,3,3,3]{1,0,4,3,2:T(4,128)} copy(f32[4,32,3,3,3]{1,0,4,3,2:T(4,128)S(1)} %bitcast.15) | data formatting | bytes 27648
  56.0 0.8 %copy.14 = f32[32,32,3,3,3]{1,0,4,3,2:T(8,128)} copy(f32[32,32,3,3,3]{1,0,4,3,2:T(8,128)S(1)} %bitcast.12) | data formatting | bytes 221184
  56.8 0.8 %copy.15 = bf16[32,2,16,256]{3,2,1,0:T(8,128)(2,1)} copy(bf16[32,2,16,256]{3,2,1,0:T(8,128)(2,1)S(1)} %get-tuple-element.19) | data formatting | bytes 1048576
Async XLA Ops:
  0.6 1.0 %copy-start = (bf16[32,2,16,256]{3,2,1,0:T(8,128)(2,1)S(1)}, bf16[32,2,16,256]{3,2,1,0:T(8,128)(2,1)}, u32[]{:S(2)}) copy-start(bf16[32,2,16,256]{3,2,1,0:T(8,128)(2,1)} %vol.1) | copy-start | bytes 1572868
  1.7 0.9 %copy-start.1 = (bf16[32,32,3,3,3]{1,0,4,3,2:T(8,128)(2,1)S(1)}, bf16[32,32,3,3,3]{1,0,4,3,2:T(8,128)(2,1)}, u32[]{:S(2)}) copy-start(bf16[32,32,3,3,3]{1,0,4,3,2:T(8,128)(2,1)} %param.5) | copy-start | bytes 165892
  2.6 0.9 %copy-start.2 = (bf16[64,32,3,3,3]{0,1,4,3,2:T(8,128)(2,1)S(1)}, bf16[64,32,3,3,3]{0,1,4,3,2:T(8,128)(2,1)}, u32[]{:S(2)}) copy-start(bf16[64,32,3,3,3]{0,1,4,3,2:T(8,128)(2,1)} %param.6) | copy-start | bytes 331780
  3.5 0.9 %copy-start.3 = (bf16[64,1,8,128]{3,2,1,0:T(8,128)(2,1)S(1)}, bf16[64,1,8,128]{3,2,1,0:T(8,128)(2,1)}, u32[]{:S(2)}) copy-start(bf16[64,1,8,128]{3,2,1,0:T(8,128)(2,1)} %cot.1) | copy-start | bytes 393220
where the time goes:
time: 57.8 us; the launch traced here: 57.6 us
  Pallas kernels  50.3 us (87%)
  local copies, waits for them, and re-layouts  6.64 us (11%)
  between operations  0.65 us (1%)
    pallas_call x1, Pallas kernels, local(): pl.pallas_call(functools.partial(kernel, n), out_shape=(jax.ShapeDtypeStr...  50.3 us
    unnamed x12, local copies, waits for them, and re-layouts  6.64 us

commit v1 on v0

v1 whole, which is shorter than its diff:
```python
import functools

import jax
import jax.numpy as jnp
from jax import lax
from jax.experimental import pallas as pl
from jax.experimental.pallas import tpu as pltpu
from jax.sharding import PartitionSpec as P

F32 = jnp.float32
BF16 = jnp.bfloat16
MESH = pl.DeviceIdType.MESH
NN = (((1,), (0,)), ((), ()))
NT = (((1,), (1,)), ((), ()))


def dot(a, b, dims=NN):
    return lax.dot_general(a, b, dims, preferred_element_type=F32)


def eye(n):
    return (
        lax.broadcasted_iota(jnp.int32, (n, n), 0) == lax.broadcasted_iota(jnp.int32, (n, n), 1)
    ).astype(BF16)


def lane_concat(parts):
    return jnp.concatenate([part.astype(F32) for part in parts], axis=1).astype(BF16)


def lanes(x, period):
    return lax.rem(lax.broadcasted_iota(jnp.int32, x.shape, 1), period)


def before_of(x, period):
    return jnp.where(lanes(x, period) == 0, 0.0, pltpu.roll(x, 1, 1))


def after_of(x, period):
    return jnp.where(lanes(x, period) == period - 1, 0.0, pltpu.roll(x, x.shape[1] - 1, 1))


def gathered(y, at, count, period, flip):
    first, mid, last = (y[at + i * count : at + (i + 1) * count] for i in range(3))
    if flip:
        first, last = last, first
    return before_of(first, period) + mid + after_of(last, period)


def rows_first(ref, value):
    for i in range(ref.shape[0]):
        ref[i] = value[:, 128 * i : 128 * (i + 1)]


def joined(ref):
    return jnp.concatenate([ref[i] for i in range(ref.shape[0])], axis=1)


def strided(ref, start, count, step):
    parts = [ref[i, pl.ds(start, count, stride=step), :] for i in range(ref.shape[0])]
    return jnp.concatenate(parts, axis=1)


def put_strided(ref, start, step, value):
    for i in range(ref.shape[0]):
        ref[i, pl.ds(start, value.shape[0], stride=step), :] = value[:, 128 * i : 128 * (i + 1)]


def zero_rims(stack):
    planes, rows, k, w = stack.shape
    for z in range(planes):
        stack[z, 0] = jnp.zeros((k, w), BF16)
        stack[z, rows - 1] = jnp.zeros((k, w), BF16)


def pair(stack, h):
    k, w = stack.shape[2:]
    rows = stack.shape[0] * 3 * k
    left = stack[:, pl.ds(h, 3)].reshape(rows, w)
    right = stack[:, pl.ds(h + 1, 3)].reshape(rows, w)
    return jnp.concatenate([left, right], axis=1)


def kernel(
    n,
    vol_in, w2_in, w3_in, cot_in,
    feat, g3, g2, gvol,
    vol, w2, w3, cot,
    xs, xb, xp, xc, bs, cs, tv, tc, slope,
    a2, b2, a3, b3, acc2, acc3, tail,
    g2send, g2recv, g2ag, g3send, g3recv,
    load, halo_send, halo_recv, s2, r2, sa, ra, s3, r3,
):
    me = lax.axis_index("gx")
    chan, planes, height, width = vol.shape
    filt, _, height_half, width_half = cot.shape
    barrier = pltpu.get_barrier_semaphore()
    loads = [
        pltpu.make_async_copy(src, dst, load.at[i])
        for i, (src, dst) in enumerate(((cot_in, cot), (vol_in, vol), (w2_in, w2), (w3_in, w3)))
    ]
    for copy in loads:
        copy.start()

    def peer(j):
        return lax.rem(me + j, n)

    def greet(j, carry):
        pl.semaphore_signal(barrier, inc=1, device_id={"gx": peer(j)}, device_id_type=MESH)
        return carry

    lax.fori_loop(1, n, greet, 0)

    def halo(slot, up, stack):
        index = 2 * slot + (0 if up else 1)
        last = stack.shape[0] - 1
        rows = pl.ds(1, stack.shape[1] - 2)
        return pltpu.make_async_remote_copy(
            src_ref=stack.at[last - 1 if up else 1, rows],
            dst_ref=stack.at[0 if up else last, rows],
            send_sem=halo_send.at[index],
            recv_sem=halo_recv.at[index],
            device_id={"gx": lax.rem(me + (1 if up else n - 1), n)},
            device_id_type=MESH,
        )

    def halo_start(slot, stack):
        @pl.when(me < n - 1)
        def _():
            halo(slot, True, stack).start()

        @pl.when(me > 0)
        def _():
            halo(slot, False, stack).start()

    def halo_arrive(slot, stack):
        @pl.when(me > 0)
        def _():
            halo(slot, True, stack).wait_recv()

        @pl.when(me < n - 1)
        def _():
            halo(slot, False, stack).wait_recv()

    def halo_sent(slot, stack):
        @pl.when(me < n - 1)
        def _():
            halo(slot, True, stack).wait_send()

        @pl.when(me > 0)
        def _():
            halo(slot, False, stack).wait_send()

    halos = ((0, xs), (1, xc), (2, xp), (3, xb))

    loads[0].wait()
    rows_first(tc, cot[:, 0].astype(F32).reshape(filt * height_half, width_half))

    def cot_row(h, carry):
        x = strided(tc, h, filt, height_half)
        xc[1, h + 1] = x.astype(BF16)
        cs[h, 0:filt] = after_of(x, width_half).astype(BF16)
        cs[h, filt : 2 * filt] = x.astype(BF16)
        cs[h, 2 * filt : 3 * filt] = before_of(x, width_half).astype(BF16)
        return carry

    lax.fori_loop(0, height_half, cot_row, 0)
    loads[1].wait()
    for d in range(planes):
        rows_first(tv.at[d], vol[:, d].astype(F32).reshape(chan * height, width))

        def vol_row(h, carry, d=d):
            xs[d + 1, h + 1] = strided(tv.at[d], h, chan, height).astype(BF16)
            return carry

        lax.fori_loop(0, height, vol_row, 0)
    for stack in (xs, xb, xp, xc):
        zero_rims(stack)
    pl.semaphore_wait(barrier, n - 1)
    halo_start(*halos[0])
    halo_start(*halos[1])

    @pl.when(me == 0)
    def _():
        for _, stack in halos:
            stack[0] = jnp.zeros(stack.shape[1:], BF16)

    @pl.when(me == n - 1)
    def _():
        for _, stack in halos:
            stack[stack.shape[0] - 1] = jnp.zeros(stack.shape[1:], BF16)

    loads[2].wait()
    loads[3].wait()
    hole = jnp.zeros((chan, chan), BF16)
    gap = jnp.zeros((chan, 4 * chan), BF16)
    for e in range(2):
        for i in range(3):
            ahead, back = [], []
            for dz in range(3):
                for y in range(4):
                    inside = 0 <= y - e <= 2
                    ahead.append(w2[9 * dz + 3 * (y - e) + i] if inside else hole)
                    back.append(w2[9 * (2 - dz) + 3 * (2 - y + e) + i] if inside else hole)
            group = lane_concat(ahead)
            flipped = dot(eye(chan), jnp.concatenate(back, axis=0), NT).astype(BF16)
            for d in range(planes):
                rows = slice(((2 * d + e) * 3 + i) * chan, ((2 * d + e) * 3 + i + 1) * chan)
                for big, part in ((a2, group), (b2, flipped)):
                    line = [gap] * d + [part] + [gap] * (planes - 1 - d)
                    big[rows, :] = jnp.concatenate(line, axis=1)
    for i in range(3):
        taps_in = [w3[3 * t + i] for t in range(9)]
        taps_out = [w3[3 * (8 - t) + i] for t in range(9)]
        b3[i * chan : (i + 1) * chan, :] = lane_concat(taps_out)
        a3[i * filt : (i + 1) * filt, :] = dot(
            eye(filt), jnp.concatenate(taps_in, axis=0), NT
        ).astype(BF16)

    fine = lax.broadcasted_iota(jnp.int32, (width, width_half), 0)
    coarse = lax.broadcasted_iota(jnp.int32, (width, width_half), 1)
    pool = ((fine == 2 * coarse) | (fine == 2 * coarse + 1)).astype(BF16)

    halo_arrive(*halos[0])

    def forward(hc, carry):
        x = xs[:, pl.ds(2 * hc, 4)].reshape((planes + 2) * 4 * chan, width)
        y = dot(a2[...], x)
        total = jnp.zeros((chan, width), F32)
        for d in range(planes):
            for e in range(2):
                before = gathered(y, (2 * d + e) * 3 * chan, chan, width, False)
                sigma = jax.nn.sigmoid(before)
                slope[d, 2 * hc + e] = sigma * (1.0 + before * (1.0 - sigma)) * 0.125
                total = total + (before * sigma).astype(BF16).astype(F32)
        high = total.astype(BF16)
        low = (total - high.astype(F32)).astype(BF16)
        xp[1, hc + 1] = ((dot(high, pool) + dot(low, pool)) * 0.125).astype(BF16)
        return carry

    lax.fori_loop(0, height_half, forward, 0)
    halo_arrive(*halos[1])
    halo_start(*halos[2])

    def backward(hq, carry):
        y = dot(b3[...], pair(xc, 2 * hq))
        back = gathered(y, 0, chan, width_half, True).astype(BF16)
        for q in range(2):
            spread = dot(back[:, q * width_half : (q + 1) * width_half], pool, NT)
            for d in range(planes):
                for e in range(2):
                    h = 4 * hq + 2 * q + e
                    value = (spread * slope[d, h]).astype(BF16)
                    wide = value.astype(F32)
                    xb[d + 1, h + 1] = value
                    bs[d, h, 0:chan] = after_of(wide, width).astype(BF16)
                    bs[d, h, chan : 2 * chan] = value
                    bs[d, h, 2 * chan : 3 * chan] = before_of(wide, width).astype(BF16)
        return carry

    lax.fori_loop(0, height_half // 2, backward, 0)

    def weight_two(h, total):
        for d in range(planes):
            x = xs[d : d + 3, pl.ds(h, 3)].reshape(9 * chan, width)
            total = total + dot(bs[d, h], x, NT)
        return total

    acc2[...] = weight_two(0, jnp.zeros(acc2.shape, F32))
    halo_start(*halos[3])

    def more_two(h, carry):
        acc2[...] = weight_two(h, acc2[...])
        return carry

    lax.fori_loop(1, height, more_two, 0)

    full = acc2.shape[1] // 128
    rest = acc2.shape[1] - 128 * full
    groups = acc2.shape[0] // 8
    units = full * groups + chan // 8
    per = g2send.shape[1] // 8
    tail[...] = jnp.concatenate(
        [acc2[i * chan : (i + 1) * chan, 128 * full :] for i in range(3)]
        + [jnp.zeros((chan, 128 - 3 * rest), F32)],
        axis=1,
    )

    def place(u):
        j, r = u // groups, u % groups
        if j == full:
            return tail, (slice(8 * r, 8 * r + 8), slice(0, 128))
        return acc2, (slice(8 * r, 8 * r + 8), slice(128 * j, 128 * j + 128))

    for u in range(n * per):
        at = (u // per, slice(u % per * 8, u % per * 8 + 8))
        if u < units:
            ref, where = place(u)
            g2send[at] = ref[where]
        else:
            g2send[at] = jnp.zeros((8, 128), F32)

    def scatter(send, recv, ssem, rsem, k, s):
        return pltpu.make_async_remote_copy(
            src_ref=send.at[k],
            dst_ref=recv.at[s],
            send_sem=ssem.at[k],
            recv_sem=rsem.at[s],
            device_id={"gx": k},
            device_id_type=MESH,
        )

    def start_all(send, recv, ssem, rsem):
        def one(j, carry):
            scatter(send, recv, ssem, rsem, peer(j), me).start()
            return carry

        lax.fori_loop(1, n, one, 0)

    def wait_sends(send, recv, ssem, rsem):
        def one(j, carry):
            scatter(send, recv, ssem, rsem, peer(j), me).wait_send()
            return carry

        lax.fori_loop(1, n, one, 0)

    def sum_all(send, recv, ssem, rsem):
        def one(j, total):
            s = peer(j)
            scatter(send, recv, ssem, rsem, s, s).wait_recv()
            return total + recv[s]

        return lax.fori_loop(1, n, one, send[me])

    halo_arrive(*halos[2])
    start_all(g2send, g2recv, s2, r2)

    acc3[...] = jnp.zeros(acc3.shape, F32)

    def weight_three(hq, carry):
        upstream = jnp.concatenate([cs[2 * hq], cs[2 * hq + 1]], axis=1)
        acc3[...] += dot(upstream, pair(xp, 2 * hq), NT)
        return carry

    lax.fori_loop(0, height_half // 2, weight_three, 0)
    own = filt // n
    for k in range(n):
        for i in range(3):
            g3send[k, i] = acc3[i * filt + k * own : i * filt + (k + 1) * own, :]

    def features(hq, carry):
        y = gathered(dot(a3[...], pair(xp, 2 * hq)), 0, filt, width_half, False)
        for q in range(2):
            put_strided(tc, 2 * hq + q, height_half, y[:, q * width_half : (q + 1) * width_half])
        return carry

    lax.fori_loop(0, height_half // 2, features, 0)
    feat[:, 0] = joined(tc).reshape(filt, height_half, width_half).astype(BF16)
    start_all(g3send, g3recv, s3, r3)

    g2ag[me] = sum_all(g2send, g2recv, s2, r2)
    halo_arrive(*halos[3])

    def gather(k, s):
        return pltpu.make_async_remote_copy(
            src_ref=g2ag.at[s],
            dst_ref=g2ag.at[s],
            send_sem=sa.at[k],
            recv_sem=ra.at[s],
            device_id={"gx": k},
            device_id_type=MESH,
        )

    def gather_start(j, carry):
        gather(peer(j), me).start()
        return carry

    lax.fori_loop(1, n, gather_start, 0)

    def volume_row(hc, carry):
        x = xb[:, pl.ds(2 * hc, 4)].reshape((planes + 2) * 4 * chan, width)
        y = dot(b2[...], x)
        for d in range(planes):
            for e in range(2):
                value = gathered(y, (2 * d + e) * 3 * chan, chan, width, True)
                put_strided(tv.at[d], 2 * hc + e, height, value)
        return carry

    lax.fori_loop(0, height_half, volume_row, 0)
    for d in range(planes):
        gvol[:, d] = joined(tv.at[d]).reshape(chan, height, width).astype(BF16)

    total = sum_all(g3send, g3recv, s3, r3)
    for t in range(27):
        g3[t] = total[t % 3, :, chan * (t // 3) : chan * (t // 3 + 1)]

    def gather_wait(j, carry):
        gather(peer(j), peer(j)).wait_recv()
        return carry

    lax.fori_loop(1, n, gather_wait, 0)
    for u in range(units):
        ref, where = place(u)
        ref[where] = g2ag[u // per, u % per * 8 : u % per * 8 + 8]
    for t in range(27):
        i, j = t % 3, t // 3
        if chan * j < 128 * full:
            g2[t] = acc2[i * chan : (i + 1) * chan, chan * j : chan * (j + 1)]
        else:
            g2[t] = tail[:, i * rest : (i + 1) * rest]

    for item in halos:
        halo_sent(*item)
    wait_sends(g2send, g2recv, s2, r2)
    wait_sends(g3send, g3recv, s3, r3)

    def gather_sent(j, carry):
        gather(peer(j), me).wait_send()
        return carry

    lax.fori_loop(1, n, gather_sent, 0)


def local(n, volume, weight_two, weight_three, cotangent):
    chan, planes, height, width = volume.shape
    filt, _, height_half, width_half = cotangent.shape
    taps = 27
    w2 = jnp.transpose(weight_two, (2, 3, 4, 0, 1)).reshape(taps, chan, chan)
    w3 = jnp.transpose(weight_three, (2, 3, 4, 1, 0)).reshape(taps, chan, filt)
    units = 3 * chan // 8 * (9 * chan // 128) + chan // 8
    per = -(-units // n)
    own = filt // n
    wide = (planes + 2) * 4 * chan
    tall = planes * 2 * 3 * chan
    dma = pltpu.SemaphoreType.DMA
    vmem = pl.BlockSpec(memory_space=pltpu.VMEM)
    hbm = pl.BlockSpec(memory_space=pltpu.HBM)
    feat, g3, g2, gvol = pl.pallas_call(
        functools.partial(kernel, n),
        out_shape=(
            jax.ShapeDtypeStruct(cotangent.shape, BF16),
            jax.ShapeDtypeStruct((taps, own, chan), F32),
            jax.ShapeDtypeStruct((taps, chan, chan), F32),
            jax.ShapeDtypeStruct(volume.shape, BF16),
        ),
        in_specs=[hbm] * 4,
        out_specs=(vmem,) * 4,
        scratch_shapes=[
            pltpu.VMEM(volume.shape, BF16),
            pltpu.VMEM(w2.shape, BF16),
            pltpu.VMEM(w3.shape, BF16),
            pltpu.VMEM(cotangent.shape, BF16),
            pltpu.VMEM((planes + 2, height + 2, chan, width), BF16),
            pltpu.VMEM((planes + 2, height + 2, chan, width), BF16),
            pltpu.VMEM((3, height_half + 2, chan, width_half), BF16),
            pltpu.VMEM((3, height_half + 2, filt, width_half), BF16),
            pltpu.VMEM((planes, height, 3 * chan, width), BF16),
            pltpu.VMEM((height_half, 3 * filt, width_half), BF16),
            pltpu.VMEM((planes, width // 128, chan * height, 128), F32),
            pltpu.VMEM((width_half // 128, filt * height_half, 128), F32),
            pltpu.VMEM((planes, height, chan, width), F32),
            pltpu.VMEM((tall, wide), BF16),
            pltpu.VMEM((tall, wide), BF16),
            pltpu.VMEM((3 * filt, 9 * chan), BF16),
            pltpu.VMEM((3 * chan, 9 * filt), BF16),
            pltpu.VMEM((3 * chan, 9 * chan), F32),
            pltpu.VMEM((3 * filt, 9 * chan), F32),
            pltpu.VMEM((chan, 128), F32),
            pltpu.VMEM((n, per * 8, 128), F32),
            pltpu.VMEM((n, per * 8, 128), F32),
            pltpu.VMEM((n, per * 8, 128), F32),
            pltpu.VMEM((n, 3, own, 9 * chan), F32),
            pltpu.VMEM((n, 3, own, 9 * chan), F32),
            dma((4,)), dma((8,)), dma((8,)),
            dma((n,)), dma((n,)), dma((n,)), dma((n,)), dma((n,)), dma((n,)),
        ],
        compiler_params=pltpu.CompilerParams(
            collective_id=0, has_side_effects=True, vmem_limit_bytes=48 << 20
        ),
    )(volume, w2, w3, cotangent)

    def taps_last(grad):
        return jnp.transpose(grad.reshape(3, 3, 3, *grad.shape[1:]), (3, 4, 0, 1, 2))

    return feat, taps_last(g3), taps_last(g2), gvol


def solution(mesh):
    return jax.shard_map(
        functools.partial(local, mesh.shape["gx"]),
        mesh=mesh,
        in_specs=(
            P(None, ("groups", "gx"), None, None),
            P(),
            P(),
            P(None, ("groups", "gx"), None, None),
        ),
        out_specs=(
            P(None, ("groups", "gx"), None, None),
            P(("groups", "gx"), None, None, None, None),
            P("groups", None, None, None, None),
            P(None, ("groups", "gx"), None, None),
        ),
        check_vma=False,
    )
```

time: 57.8 us -> 46 us (0.80)
  Pallas kernels: 50.3 us -> 38.5 us
    pallas_call x1, Pallas kernels: 50.3 us -> 38.5 us  [local(): pl.pallas_call(functools.partial(kernel, n), out_shape=(jax.ShapeDtypeStr...]
where the time goes in v1:
time: 46 us; the launch traced here: 45.8 us
  Pallas kernels  38.5 us (84%)
  local copies, waits for them, and re-layouts  6.64 us (14%)
  between operations  0.65 us (1%)
    pallas_call x1, Pallas kernels, local(): pl.pallas_call(functools.partial(kernel, n), out_shape=(jax.ShapeDtypeStr...  38.5 us
    unnamed x12, local copies, waits for them, and re-layouts  6.64 us

profile of v1, /device:TPU:0, one launch (start us, length us, event | category | flops | bytes accessed | tf_op | source)
XLA Modules:
  0.0 45.8 jit_solution(11501076695534398015)
XLA Ops:
  0.6 0.0 copy-start
  0.6 1.0 %copy-done = bf16[32,2,16,256]{3,2,1,0:T(8,128)(2,1)S(1)} copy-done((bf16[32,2,16,256]{3,2,1,0:T(8,128)(2,1)S(1)}, bf16[32,2,16,256]{3,2,1,0:T(8,128)(2,1)}, u32[]{:S(2)}) %copy-start) | copy-done | bytes 524312
  1.7 0.0 copy-start.1
  1.7 0.9 %copy-done.1 = bf16[32,32,3,3,3]{1,0,4,3,2:T(8,128)(2,1)S(1)} copy-done((bf16[32,32,3,3,3]{1,0,4,3,2:T(8,128)(2,1)S(1)}, bf16[32,32,3,3,3]{1,0,4,3,2:T(8,128)(2,1)}, u32[]{:S(2)}) %copy-start.1) | copy-done | bytes 55320
  2.6 0.0 copy-start.2
  2.6 0.9 %copy-done.2 = bf16[64,32,3,3,3]{0,1,4,3,2:T(8,128)(2,1)S(1)} copy-done((bf16[64,32,3,3,3]{0,1,4,3,2:T(8,128)(2,1)S(1)}, bf16[64,32,3,3,3]{0,1,4,3,2:T(8,128)(2,1)}, u32[]{:S(2)}) %copy-start.2) | copy-done | bytes 110616
  3.5 0.0 copy-start.3
  3.5 0.9 %copy-done.3 = bf16[64,1,8,128]{3,2,1,0:T(8,128)(2,1)S(1)} copy-done((bf16[64,1,8,128]{3,2,1,0:T(8,128)(2,1)S(1)}, bf16[64,1,8,128]{3,2,1,0:T(8,128)(2,1)}, u32[]{:S(2)}) %copy-start.3) | copy-done | bytes 131096
  4.5 38.5 %shard_map.75 = (bf16[64,1,8,128]{3,2,1,0:T(8,128)(2,1)S(1)}, f32[27,4,32]{2,1,0:T(4,128)S(1)}, f32[27,32,32]{2,1,0:T(8,128)S(1)}, bf16[32,2,16,256]{3,2,1,0:T(8,128)(2,1)S(1)}) custom-call(bf16[32,2,16,256]{3,2,1,0:T(8,128)(2,1)S(1)} %copy-done, bf16[27,32,32]{2,1,0:T(8,128)(2,1)S(1)} %bitcast.13, bf16[27,32,64]{2,1,0:T(8,128)(2,1)S(1)} %bitcast.14, ...), custom_call_target="tpu_custom_call" | custom-call | tf_op jit(solution)/shard_map/pallas_call | solution.py:438
  43.0 0.7 %copy.12 = bf16[64,1,8,128]{3,2,1,0:T(8,128)(2,1)} copy(bf16[64,1,8,128]{3,2,1,0:T(8,128)(2,1)S(1)} %get-tuple-element.16) | data formatting | bytes 262144
  43.6 0.6 %copy.13 = f32[4,32,3,3,3]{1,0,4,3,2:T(4,128)} copy(f32[4,32,3,3,3]{1,0,4,3,2:T(4,128)S(1)} %bitcast.15) | data formatting | bytes 27648
  44.3 0.8 %copy.14 = f32[32,32,3,3,3]{1,0,4,3,2:T(8,128)} copy(f32[32,32,3,3,3]{1,0,4,3,2:T(8,128)S(1)} %bitcast.12) | data formatting | bytes 221184
  45.0 0.8 %copy.15 = bf16[32,2,16,256]{3,2,1,0:T(8,128)(2,1)} copy(bf16[32,2,16,256]{3,2,1,0:T(8,128)(2,1)S(1)} %get-tuple-element.19) | data formatting | bytes 1048576
Async XLA Ops:
  0.6 1.0 %copy-start = (bf16[32,2,16,256]{3,2,1,0:T(8,128)(2,1)S(1)}, bf16[32,2,16,256]{3,2,1,0:T(8,128)(2,1)}, u32[]{:S(2)}) copy-start(bf16[32,2,16,256]{3,2,1,0:T(8,128)(2,1)} %vol_in.1) | copy-start | bytes 1572868
  1.7 0.9 %copy-start.1 = (bf16[32,32,3,3,3]{1,0,4,3,2:T(8,128)(2,1)S(1)}, bf16[32,32,3,3,3]{1,0,4,3,2:T(8,128)(2,1)}, u32[]{:S(2)}) copy-start(bf16[32,32,3,3,3]{1,0,4,3,2:T(8,128)(2,1)} %param.5) | copy-start | bytes 165892
  2.6 0.9 %copy-start.2 = (bf16[64,32,3,3,3]{0,1,4,3,2:T(8,128)(2,1)S(1)}, bf16[64,32,3,3,3]{0,1,4,3,2:T(8,128)(2,1)}, u32[]{:S(2)}) copy-start(bf16[64,32,3,3,3]{0,1,4,3,2:T(8,128)(2,1)} %param.6) | copy-start | bytes 331780
  3.5 0.9 %copy-start.3 = (bf16[64,1,8,128]{3,2,1,0:T(8,128)(2,1)S(1)}, bf16[64,1,8,128]{3,2,1,0:T(8,128)(2,1)}, u32[]{:S(2)}) copy-start(bf16[64,1,8,128]{3,2,1,0:T(8,128)(2,1)} %cot_in.1) | copy-start | bytes 393220

commit v2 on v1

--- a/solution.py
+++ b/solution.py
@@ -86,7 +86,7 @@
     vol_in, w2_in, w3_in, cot_in,
     feat, g3, g2, gvol,
     vol, w2, w3, cot,
-    xs, xb, xp, xc, bs, cs, tv, tc, slope,
+    xs, xb, xp, xc, bs, cs, tv, tc, backs,
     a2, b2, a3, b3, acc2, acc3, tail,
     g2send, g2recv, g2ag, g3send, g3recv,
     load, halo_send, halo_recv, s2, r2, sa, ra, s3, r3,
@@ -111,10 +111,11 @@
 
     lax.fori_loop(1, n, greet, 0)
 
-    def halo(slot, up, stack):
+    def halo(slot, stack, part, parts, up):
         index = 2 * slot + (0 if up else 1)
         last = stack.shape[0] - 1
-        rows = pl.ds(1, stack.shape[1] - 2)
+        count = (stack.shape[1] - 2) // parts
+        rows = pl.ds(1 + part * count, count)
         return pltpu.make_async_remote_copy(
             src_ref=stack.at[last - 1 if up else 1, rows],
             dst_ref=stack.at[0 if up else last, rows],
@@ -124,34 +125,36 @@
             device_id_type=MESH,
         )
 
-    def halo_start(slot, stack):
+    def halo_start(*item):
         @pl.when(me < n - 1)
         def _():
-            halo(slot, True, stack).start()
+            halo(*item, True).start()
 
         @pl.when(me > 0)
         def _():
-            halo(slot, False, stack).start()
-
-    def halo_arrive(slot, stack):
+            halo(*item, False).start()
+
+    def halo_arrive(*item):
         @pl.when(me > 0)
         def _():
-            halo(slot, True, stack).wait_recv()
+            halo(*item, True).wait_recv()
 
         @pl.when(me < n - 1)
         def _():
-            halo(slot, False, stack).wait_recv()
-
-    def halo_sent(slot, stack):
+            halo(*item, False).wait_recv()
+
+    def halo_sent(*item):
         @pl.when(me < n - 1)
         def _():
-            halo(slot, True, stack).wait_send()
+            halo(*item, True).wait_send()
 
         @pl.when(me > 0)
         def _():
-            halo(slot, False, stack).wait_send()
-
-    halos = ((0, xs), (1, xc), (2, xp), (3, xb))
+            halo(*item, False).wait_send()
+
+    halos = (
+        (0, xs, 0, 2), (1, xs, 1, 2), (2, xc, 0, 1), (3, xp, 0, 1), (4, xb, 0, 2), (5, xb, 1, 2)
+    )
 
     loads[0].wait()
     rows_first(tc, cot[:, 0].astype(F32).reshape(filt * height_half, width_half))
@@ -177,17 +180,18 @@
     for stack in (xs, xb, xp, xc):
         zero_rims(stack)
     pl.semaphore_wait(barrier, n - 1)
+    halo_start(*halos[2])
     halo_start(*halos[0])
     halo_start(*halos[1])
 
     @pl.when(me == 0)
     def _():
-        for _, stack in halos:
+        for stack in (xs, xb, xp, xc):
             stack[0] = jnp.zeros(stack.shape[1:], BF16)
 
     @pl.when(me == n - 1)
     def _():
-        for _, stack in halos:
+        for stack in (xs, xb, xp, xc):
             stack[stack.shape[0] - 1] = jnp.zeros(stack.shape[1:], BF16)
 
     loads[2].wait()
@@ -221,44 +225,44 @@
     coarse = lax.broadcasted_iota(jnp.int32, (width, width_half), 1)
     pool = ((fine == 2 * coarse) | (fine == 2 * coarse + 1)).astype(BF16)
 
-    halo_arrive(*halos[0])
+    halo_arrive(*halos[2])
+
+    def coarse_back(hq, carry):
+        y = dot(b3[...], pair(xc, 2 * hq))
+        value = gathered(y, 0, chan, width_half, True).astype(BF16)
+        for q in range(2):
+            backs[2 * hq + q] = value[:, q * width_half : (q + 1) * width_half]
+        return carry
+
+    lax.fori_loop(0, height_half // 2, coarse_back, 0)
 
     def forward(hc, carry):
         x = xs[:, pl.ds(2 * hc, 4)].reshape((planes + 2) * 4 * chan, width)
         y = dot(a2[...], x)
+        spread = dot(backs[hc], pool, NT) * 0.125
         total = jnp.zeros((chan, width), F32)
         for d in range(planes):
             for e in range(2):
+                h = 2 * hc + e
                 before = gathered(y, (2 * d + e) * 3 * chan, chan, width, False)
                 sigma = jax.nn.sigmoid(before)
-                slope[d, 2 * hc + e] = sigma * (1.0 + before * (1.0 - sigma)) * 0.125
                 total = total + (before * sigma).astype(BF16).astype(F32)
+                value = (spread * (sigma * (1.0 + before * (1.0 - sigma)))).astype(BF16)
+                wide = value.astype(F32)
+                xb[d + 1, h + 1] = value
+                bs[d, h, 0:chan] = after_of(wide, width).astype(BF16)
+                bs[d, h, chan : 2 * chan] = value
+                bs[d, h, 2 * chan : 3 * chan] = before_of(wide, width).astype(BF16)
         high = total.astype(BF16)
         low = (total - high.astype(F32)).astype(BF16)
         xp[1, hc + 1] = ((dot(high, pool) + dot(low, pool)) * 0.125).astype(BF16)
         return carry
 
-    lax.fori_loop(0, height_half, forward, 0)
+    ready = height_half // 2 - 1
+    halo_arrive(*halos[0])
+    lax.fori_loop(0, ready, forward, 0)
     halo_arrive(*halos[1])
-    halo_start(*halos[2])
-
-    def backward(hq, carry):
-        y = dot(b3[...], pair(xc, 2 * hq))
-        back = gathered(y, 0, chan, width_half, True).astype(BF16)
-        for q in range(2):
-            spread = dot(back[:, q * width_half : (q + 1) * width_half], pool, NT)
-            for d in range(planes):
-                for e in range(2):
-                    h = 4 * hq + 2 * q + e
-                    value = (spread * slope[d, h]).astype(BF16)
-                    wide = value.astype(F32)
-                    xb[d + 1, h + 1] = value
-                    bs[d, h, 0:chan] = after_of(wide, width).astype(BF16)
-                    bs[d, h, chan : 2 * chan] = value
-                    bs[d, h, 2 * chan : 3 * chan] = before_of(wide, width).astype(BF16)
-        return carry
-
-    lax.fori_loop(0, height_half // 2, backward, 0)
+    lax.fori_loop(ready, height_half, forward, 0)
 
     def weight_two(h, total):
         for d in range(planes):
@@ -268,6 +272,8 @@
 
     acc2[...] = weight_two(0, jnp.zeros(acc2.shape, F32))
     halo_start(*halos[3])
+    halo_start(*halos[4])
+    halo_start(*halos[5])
 
     def more_two(h, carry):
         acc2[...] = weight_two(h, acc2[...])
@@ -332,7 +338,7 @@
 
         return lax.fori_loop(1, n, one, send[me])
 
-    halo_arrive(*halos[2])
+    halo_arrive(*halos[3])
     start_all(g2send, g2recv, s2, r2)
 
     acc3[...] = jnp.zeros(acc3.shape, F32)
@@ -358,8 +364,19 @@
     feat[:, 0] = joined(tc).reshape(filt, height_half, width_half).astype(BF16)
     start_all(g3send, g3recv, s3, r3)
 
+    def volume_row(hc, carry):
+        x = xb[:, pl.ds(2 * hc, 4)].reshape((planes + 2) * 4 * chan, width)
+        y = dot(b2[...], x)
+        for d in range(planes):
+            for e in range(2):
+                value = gathered(y, (2 * d + e) * 3 * chan, chan, width, True)
+                put_strided(tv.at[d], 2 * hc + e, height, value)
+        return carry
+
+    halo_arrive(*halos[4])
+    lax.fori_loop(0, ready - 1, volume_row, 0)
     g2ag[me] = sum_all(g2send, g2recv, s2, r2)
-    halo_arrive(*halos[3])
+    lax.fori_loop(ready - 1, ready, volume_row, 0)
 
     def gather(k, s):
         return pltpu.make_async_remote_copy(
@@ -377,16 +394,8 @@
 
     lax.fori_loop(1, n, gather_start, 0)
 
-    def volume_row(hc, carry):
-        x = xb[:, pl.ds(2 * hc, 4)].reshape((planes + 2) * 4 * chan, width)
-        y = dot(b2[...], x)
-        for d in range(planes):
-            for e in range(2):
-                value = gathered(y, (2 * d + e) * 3 * chan, chan, width, True)
-                put_strided(tv.at[d], 2 * hc + e, height, value)
-        return carry
-
-    lax.fori_loop(0, height_half, volume_row, 0)
+    halo_arrive(*halos[5])
+    lax.fori_loop(ready, height_half, volume_row, 0)
     for d in range(planes):
         gvol[:, d] = joined(tv.at[d]).reshape(chan, height, width).astype(BF16)
 
@@ -458,7 +467,7 @@
             pltpu.VMEM((height_half, 3 * filt, width_half), BF16),
             pltpu.VMEM((planes, width // 128, chan * height, 128), F32),
             pltpu.VMEM((width_half // 128, filt * height_half, 128), F32),
-            pltpu.VMEM((planes, height, chan, width), F32),
+            pltpu.VMEM((height_half, chan, width_half), BF16),
             pltpu.VMEM((tall, wide), BF16),
             pltpu.VMEM((tall, wide), BF16),
             pltpu.VMEM((3 * filt, 9 * chan), BF16),
@@ -471,11 +480,11 @@
             pltpu.VMEM((n, per * 8, 128), F32),
             pltpu.VMEM((n, 3, own, 9 * chan), F32),
             pltpu.VMEM((n, 3, own, 9 * chan), F32),
-            dma((4,)), dma((8,)), dma((8,)),
+            dma((4,)), dma((12,)), dma((12,)),
             dma((n,)), dma((n,)), dma((n,)), dma((n,)), dma((n,)), dma((n,)),
         ],
         compiler_params=pltpu.CompilerParams(
-            collective_id=0, has_side_effects=True, vmem_limit_bytes=48 << 20
+            collective_id=0, has_side_effects=True, vmem_limit_bytes=67043328
         ),
     )(volume, w2, w3, cotangent)
 

time: 46 us -> 43.3 us (0.941)
  local copies, waits for them, and re-layouts: 6.64 us -> 4.81 us
  Pallas kernels: 38.5 us -> 37.7 us
    unnamed x12 -> x8, local copies, waits for them, and re-layouts: 6.64 us -> 4.81 us
    pallas_call x1, Pallas kernels: 38.5 us -> 37.7 us  [local(): pl.pallas_call(functools.partial(kernel, n), out_shape=(jax.ShapeDtypeStr...]
where the time goes in v2:
time: 43.3 us; the launch traced here: 43.1 us
  Pallas kernels  37.7 us (87%)
  local copies, waits for them, and re-layouts  4.81 us (11%)
  between operations  0.65 us (2%)
    pallas_call x1, Pallas kernels, local(): pl.pallas_call(functools.partial(kernel, n), out_shape=(jax.ShapeDtypeStr...  37.7 us
    unnamed x8, local copies, waits for them, and re-layouts  4.81 us

profile of v2, /device:TPU:0, one launch (start us, length us, event | category | flops | bytes accessed | tf_op | source)
XLA Modules:
  0.0 43.1 jit_solution(4178903294139863087)
XLA Ops:
  0.6 37.7 %shard_map.75 = (bf16[64,1,8,128]{3,2,1,0:T(8,128)(2,1)}, f32[27,4,32]{2,1,0:T(4,128)}, f32[27,32,32]{2,1,0:T(8,128)}, bf16[32,2,16,256]{3,2,1,0:T(8,128)(2,1)}) custom-call(bf16[32,2,16,256]{3,2,1,0:T(8,128)(2,1)} %vol_in.1, bf16[27,32,32]{2,1,0:T(8,128)(2,1)} %bitcast.13, bf16[27,32,64]{2,1,0:T(8,128)(2,1)} %bitcast.14, bf16[64,1,8,128]{3,2,1,0:T(8,128)(2,1)} %cot_in.1), custom_call_target="tpu_custom_call" | custom-call | tf_op jit(solution)/shard_map/pallas_call | solution.py:447
  38.3 0.0 copy-start.1
  38.3 1.6 %copy.12 = bf16[64,1,8,128]{3,2,1,0:T(8,128)(2,1)} copy(bf16[64,1,8,128]{3,2,1,0:T(8,128)(2,1)} %get-tuple-element.16) | data formatting | bytes 262144
  39.9 0.0 copy-done.1
  39.9 0.0 copy-start
  39.9 0.6 %copy.13 = f32[4,32,3,3,3]{1,0,4,3,2:T(4,128)} copy(f32[4,32,3,3,3]{1,0,4,3,2:T(4,128)S(1)} %bitcast.15) | data formatting | bytes 27648
  40.5 1.8 %copy.14 = f32[32,32,3,3,3]{1,0,4,3,2:T(8,128)} copy(f32[32,32,3,3,3]{1,0,4,3,2:T(8,128)} %bitcast.12) | data formatting | bytes 221184
  42.4 0.0 copy-done
  42.4 0.8 %copy.15 = bf16[32,2,16,256]{3,2,1,0:T(8,128)(2,1)} copy(bf16[32,2,16,256]{3,2,1,0:T(8,128)(2,1)S(1)} %copy-done) | data formatting | bytes 1048576
Async XLA Ops:
  38.3 1.6 %copy-start.1 = (f32[27,4,32]{2,1,0:T(4,128)S(1)}, f32[27,4,32]{2,1,0:T(4,128)}, u32[]{:S(2)}) copy-start(f32[27,4,32]{2,1,0:T(4,128)} %get-tuple-element.9) | copy-start | bytes 41476
  39.9 2.4 %copy-start = (bf16[32,2,16,256]{3,2,1,0:T(8,128)(2,1)S(1)}, bf16[32,2,16,256]{3,2,1,0:T(8,128)(2,1)}, u32[]{:S(2)}) copy-start(bf16[32,2,16,256]{3,2,1,0:T(8,128)(2,1)} %get-tuple-element.19) | copy-start | bytes 1572868

commit v3 on v2

--- a/solution.py
+++ b/solution.py
@@ -361,7 +361,9 @@
         return carry
 
     lax.fori_loop(0, height_half // 2, features, 0)
-    feat[:, 0] = joined(tc).reshape(filt, height_half, width_half).astype(BF16)
+    cot[:, 0] = joined(tc).reshape(filt, height_half, width_half).astype(BF16)
+    store_feat = pltpu.make_async_copy(cot, feat, load.at[0])
+    store_feat.start()
     start_all(g3send, g3recv, s3, r3)
 
     def volume_row(hc, carry):
@@ -397,7 +399,9 @@
     halo_arrive(*halos[5])
     lax.fori_loop(ready, height_half, volume_row, 0)
     for d in range(planes):
-        gvol[:, d] = joined(tv.at[d]).reshape(chan, height, width).astype(BF16)
+        vol[:, d] = joined(tv.at[d]).reshape(chan, height, width).astype(BF16)
+    store_vol = pltpu.make_async_copy(vol, gvol, load.at[1])
+    store_vol.start()
 
     total = sum_all(g3send, g3recv, s3, r3)
     for t in range(27):
@@ -418,6 +422,8 @@
         else:
             g2[t] = tail[:, i * rest : (i + 1) * rest]
 
+    store_feat.wait()
+    store_vol.wait()
     for item in halos:
         halo_sent(*item)
     wait_sends(g2send, g2recv, s2, r2)
@@ -453,7 +459,7 @@
             jax.ShapeDtypeStruct(volume.shape, BF16),
         ),
         in_specs=[hbm] * 4,
-        out_specs=(vmem,) * 4,
+        out_specs=(hbm, vmem, vmem, hbm),
         scratch_shapes=[
             pltpu.VMEM(volume.shape, BF16),
             pltpu.VMEM(w2.shape, BF16),

time: 43.3 us -> 43.1 us (level)
  no operation moved by 1% of the time
where the time goes in v3:
time: 43.1 us; the launch traced here: 42.9 us
  Pallas kernels  37.5 us (87%)
  local copies, waits for them, and re-layouts  4.81 us (11%)
  between operations  0.65 us (2%)
    pallas_call x1, Pallas kernels, local(): pl.pallas_call(functools.partial(kernel, n), out_shape=(jax.ShapeDtypeStr...  37.5 us
    unnamed x8, local copies, waits for them, and re-layouts  4.81 us

profile of v3, /device:TPU:0, one launch (start us, length us, event | category | flops | bytes accessed | tf_op | source)
XLA Modules:
  0.0 42.9 jit_solution(14775009284399238961)
XLA Ops:
  0.6 37.5 %shard_map.75 = (bf16[64,1,8,128]{3,2,1,0:T(8,128)(2,1)}, f32[27,4,32]{2,1,0:T(4,128)}, f32[27,32,32]{2,1,0:T(8,128)}, bf16[32,2,16,256]{3,2,1,0:T(8,128)(2,1)}) custom-call(bf16[32,2,16,256]{3,2,1,0:T(8,128)(2,1)} %vol_in.1, bf16[27,32,32]{2,1,0:T(8,128)(2,1)} %bitcast.13, bf16[27,32,64]{2,1,0:T(8,128)(2,1)} %bitcast.14, bf16[64,1,8,128]{3,2,1,0:T(8,128)(2,1)} %cot_in.1), custom_call_target="tpu_custom_call" | custom-call | tf_op jit(solution)/shard_map/pallas_call | solution.py:453
  38.1 0.0 copy-start.1
  38.1 1.6 %copy.12 = bf16[64,1,8,128]{3,2,1,0:T(8,128)(2,1)} copy(bf16[64,1,8,128]{3,2,1,0:T(8,128)(2,1)} %get-tuple-element.16) | data formatting | bytes 262144
  39.7 0.0 copy-done.1
  39.7 0.0 copy-start
  39.7 0.6 %copy.13 = f32[4,32,3,3,3]{1,0,4,3,2:T(4,128)} copy(f32[4,32,3,3,3]{1,0,4,3,2:T(4,128)S(1)} %bitcast.15) | data formatting | bytes 27648
  40.3 1.8 %copy.14 = f32[32,32,3,3,3]{1,0,4,3,2:T(8,128)} copy(f32[32,32,3,3,3]{1,0,4,3,2:T(8,128)} %bitcast.12) | data formatting | bytes 221184
  42.1 0.0 copy-done
  42.1 0.8 %copy.15 = bf16[32,2,16,256]{3,2,1,0:T(8,128)(2,1)} copy(bf16[32,2,16,256]{3,2,1,0:T(8,128)(2,1)S(1)} %copy-done) | data formatting | bytes 1048576
Async XLA Ops:
  38.1 1.6 %copy-start.1 = (f32[27,4,32]{2,1,0:T(4,128)S(1)}, f32[27,4,32]{2,1,0:T(4,128)}, u32[]{:S(2)}) copy-start(f32[27,4,32]{2,1,0:T(4,128)} %get-tuple-element.9) | copy-start | bytes 41476
  39.7 2.4 %copy-start = (bf16[32,2,16,256]{3,2,1,0:T(8,128)(2,1)S(1)}, bf16[32,2,16,256]{3,2,1,0:T(8,128)(2,1)}, u32[]{:S(2)}) copy-start(bf16[32,2,16,256]{3,2,1,0:T(8,128)(2,1)} %get-tuple-element.19) | copy-start | bytes 1572868
